TPU v7x, 256 devices: a whole 4x4x8 slice. The times are simulated.
256 devices in a mesh: leaf: 64 (over x, z, core), rhs: 4 (over y).
Axes of the slice: x: 4, y: 4, z: 8, core: 2. Of those that a mesh axis runs over, the one named last changes fastest.
Arguments:
- fields: bfloat16 [131072, 1024], P('leaf', 'rhs'), may hold values from -6 to 6
- owner: int32 [131072, 1], P('leaf'), may hold values from 0 to 63; in each aligned block of 2048 rows (0 to 2047, 2048 to 4095, ...) at most 64 rows name the same one
- source_basis: bfloat16 [131072, 256], P('leaf'), may hold values from -0.125 to 0.125
- field_basis: bfloat16 [131072, 256], P('leaf'), may hold values from -0.375 to 0.375
- transfer: bfloat16 [64, 3, 256, 512], P('leaf', None, 'rhs'), may hold values from -0.25 to 0.25
- near_blocks: bfloat16 [512, 7, 256, 256], P('leaf'), may hold values from -0.25 to 0.25
- near_index: int32 [512, 7], P('leaf'), may hold values from 0 to 7
- near_count: int32 [512], P('leaf'), may hold values from 1 to 7
Outputs:
- scattered: bfloat16 [131072, 1024], P('leaf', 'rhs')
Inputs may be any that keep to these rules, and one draw needn't show every extreme that they name: In the rows of one group of 2048 rows at most 64 name one owner; in some group one owner is named by exactly 64. `near_index`: Row-block numbers counted within the same group of 8 row blocks.
All inputs are finite; a program needn't handle non-finite values.
Results may differ from a plain program's by a relative error of at most 0.006.
Values may be sent and summed in bfloat16 or wider, within the bound.
A program may use at most 128 MiB of HBM per device.

v0:
```python
import jax
import jax.numpy as jnp
from jax import lax
from jax.sharding import PartitionSpec as P


def swapped(value, axis, stride):
    return lax.ppermute(value, axis, [(i, i ^ 1 << stride) for i in range(lax.axis_size(axis))])


def slot_numbers(owners_of, n_leaf, capacity):
    onehot = (owners_of[:, None] == jnp.arange(n_leaf, dtype=jnp.int32)[None, :]).astype(jnp.int32)
    before = jnp.cumsum(onehot, axis=0) - onehot
    rank_in = jnp.sum(before * onehot, axis=1)
    return owners_of * capacity + rank_in


def on_device(
    fields, owner, source_basis, field_basis, transfer, near_blocks, near_index, near_count
):
    n_leaf = lax.axis_size("leaf")
    row_count, col_count = fields.shape
    basis_width = source_basis.shape[1]
    capacity = 2 * row_count // n_leaf
    slot_index = slot_numbers(owner[:, 0], n_leaf, capacity)
    block_rows = near_blocks.shape[2]
    block_count, near_slots = near_index.shape
    chosen = fields.reshape(block_count, block_rows, col_count)[near_index]
    keep_mask = jnp.arange(near_slots, dtype=jnp.int32)[None, :] < near_count[:, None]
    chosen = jnp.where(keep_mask[:, :, None, None], chosen, jnp.zeros((), jnp.bfloat16))
    near_term = jnp.einsum(
        "gjab,gjbn->gan", near_blocks, chosen, preferred_element_type=jnp.float32
    ).reshape(row_count, col_count)
    x_slots = jnp.zeros((n_leaf * capacity, col_count), jnp.bfloat16).at[slot_index].set(fields)
    v_slots = (
        jnp.zeros((n_leaf * capacity, basis_width), jnp.bfloat16).at[slot_index].set(source_basis)
    )
    u_slots = (
        jnp.zeros((n_leaf * capacity, basis_width), jnp.bfloat16).at[slot_index].set(field_basis)
    )
    x_three = x_slots.reshape(n_leaf, capacity, col_count)
    v_three = v_slots.reshape(n_leaf, capacity, basis_width)
    coefficients = lax.psum_scatter(
        jnp.einsum("bck,bcn->bkn", v_three, x_three, preferred_element_type=jnp.float32),
        "leaf",
        scatter_dimension=0,
        tiled=True,
    )[0].astype(jnp.bfloat16)
    for level_num in range(transfer.shape[1]):
        partner = swapped(coefficients, "leaf", level_num)
        stacked = jnp.concatenate([coefficients, partner], axis=0)

        def apply_rows(shard_piece, offset, stacked=stacked):
            return jnp.dot(shard_piece, stacked, preferred_element_type=jnp.float32)

        coefficients = apply_rows(
            lax.all_gather(transfer[0, level_num], "rhs", axis=0, tiled=True), jnp.int32(0)
        ).astype(jnp.bfloat16)
    u_three = u_slots.reshape(n_leaf, capacity, basis_width)
    far_slots = (
        jnp.einsum(
            "bck,bkn->bcn",
            u_three,
            lax.all_gather(coefficients[None], "leaf", axis=0, tiled=True),
            preferred_element_type=jnp.float32,
        )
        .astype(jnp.bfloat16)
        .reshape(n_leaf * capacity, col_count)
    )
    far_term = far_slots[slot_index]
    return (far_term.astype(jnp.float32) + near_term).astype(jnp.bfloat16)


def solution(mesh):
    in_specs = (
        P("leaf", "rhs"),
        P("leaf", None),
        P("leaf", None),
        P("leaf", None),
        P("leaf", None, "rhs", None),
        P("leaf", None, None, None),
        P("leaf", None),
        P("leaf"),
    )
    out_specs = P("leaf", "rhs")
    return jax.shard_map(
        on_device, mesh=mesh, in_specs=in_specs, out_specs=out_specs, check_vma=False
    )
```

profile of v0, /device:TPU:5, one launch (start us, length us, event | category | flops | bytes accessed | tf_op | source)
XLA Modules:
  0.0 411.8 jit_solution(9575077675460994863)
XLA Ops:
  6.5 0.0 reduce-scatter.2.cloned.1.call-start
  6.5 0.0 copy-start.2
  6.5 0.8 fusion.17
  7.3 18.1 %reduce-window.6 = s32[64,16,128]{2,1,0:T(8,128)S(1)} reduce-window(s32[64,16,128]{2,1,0:T(8,128)S(1)} %fusion.17, s32[]{:T(128)} %constant.7.clone.1), window={size=1x1x128 pad=0_0x0_0x127_0}, to_apply=%region_0.0 | reduce-window | flops 16646144 | bytes 1048580 | tf_op jit(solution)/shard_map/reduce-window
  25.5 0.2 slice.24
  25.7 0.0 copy-start
  25.7 0.4 copy.14
  26.1 0.2 reduce-window.9
  26.3 0.2 broadcast_add_fusion
  26.5 0.0 copy-done.2
  26.5 0.3 fusion.16
  26.8 10.4 %scatter_custom_fusion.1 = bf16[4096,256]{1,0:T(8,128)(2,1)S(1)} fusion(s32[2048]{0:T(1024)S(1)} %bitcast.75, bf16[2048,256]{1,0:T(8,128)(2,1)} %param.10, bf16[]{:T(256)} %constant.5.clone.1), kind=kCustom, calls=%fused_computation.20 | custom fusion | bytes 2097664 | tf_op jit(solution)/shard_map/scatter | solution.py:36
  37.2 0.0 copy-done
  37.2 10.9 %scatter_custom_fusion.2 = bf16[4096,256]{1,0:T(8,128)(2,1)} fusion(s32[2048]{0:T(1024)S(1)} %bitcast.76, bf16[2048,256]{1,0:T(8,128)(2,1)S(1)} %copy-done, bf16[]{:T(256)} %constant.5.clone.1), kind=kCustom, calls=%fused_computation.18 | custom fusion | bytes 2097154 | tf_op jit(solution)/shard_map/scatter | solution.py:34
  48.1 9.7 %fusion.35 = f32[64,256,256]{2,1,0:T(8,128)} fusion(bf16[64,64,256]{2,1,0:T(8,128)(2,1)S(1)} %bitcast.66, bf16[64,64,256]{2,1,0:T(8,128)(2,1)} %bitcast.67), kind=kOutput, calls=%fused_computation.55 | convolution fusion | flops 536870912 | bytes 20971520 | tf_op jit(solution)/shard_map/bck,bcn->bkn/dot_general | solution.py:44
  57.8 0.0 copy-start.1
  57.8 0.0 reduce-scatter.2.cloned.1.call-update
  57.8 0.0 all-gather.6.cloned.1.call-start
  57.9 187.9 %reduce-scatter.2.cloned.1.call-done = f32[1,256,256]{2,1,0:T(8,128)} async-done(((f32[64,256,256]{2,1,0:T(8,128)}), f32[1,256,256]{2,1,0:T(8,128)}) %reduce-scatter.2.cloned.1.call-update) | async-done | bytes 262160 | tf_op jit(solution)/shard_map/reduce_scatter | solution.py:43
  245.8 1.0 convert_bitcast_fusion
  246.8 4.8 %collective-permute-start = (bf16[256,256]{1,0:T(8,128)(2,1)S(1)}, bf16[256,256]{1,0:T(8,128)(2,1)S(1)}, u32[]{:S(2)}, u32[]{:S(2)}) collective-permute-start(bf16[256,256]{1,0:T(8,128)(2,1)S(1)} %convert_bitcast_fusion), channel_id=1, source_target_pairs={{0,4},{4,0},{8,12},{12,8},{16,20},{20,16},{24,28},{28,24},{32,36},... | collective-permute-start | bytes 393224 | tf_op jit(solution)/shard_map/ppermute | solution.py:8
  251.6 0.0 copy-done.1
  251.6 9.9 %all-gather = bf16[1,1,256,512]{3,2,1,0:T(8,128)(2,1)S(1)} all-gather(bf16[1,1,64,512]{3,2,1,0:T(8,128)(2,1)S(1)} %get-tuple-element.6), channel_id=2, replica_groups=mesh['leaf'=64,'rhs'=4] {'rhs'}, dimensions={2}, use_global_device_ids=true | all-gather | bytes 327680 | tf_op jit(solution)/shard_map/all_gather | solution.py:57
  261.5 0.0 collective-permute-done
  261.5 0.2 fusion.6
  261.8 0.8 collective-permute-start.1
  262.6 9.4 %all-gather.1 = bf16[1,1,256,512]{3,2,1,0:T(8,128)(2,1)S(1)} all-gather(bf16[1,1,64,512]{3,2,1,0:T(8,128)(2,1)S(1)} %get-tuple-element.7), channel_id=3, replica_groups=mesh['leaf'=64,'rhs'=4] {'rhs'}, dimensions={2}, use_global_device_ids=true | all-gather | bytes 327680 | tf_op jit(solution)/shard_map/all_gather | solution.py:57
  271.9 0.0 copy-start.3
  272.0 0.0 collective-permute-done.1
  272.0 0.2 fusion.7
  272.2 2.6 collective-permute-start.2
  274.8 9.5 %all-gather.2 = bf16[1,1,256,512]{3,2,1,0:T(8,128)(2,1)S(1)} all-gather(bf16[1,1,64,512]{3,2,1,0:T(8,128)(2,1)S(1)} %get-tuple-element.5), channel_id=4, replica_groups=mesh['leaf'=64,'rhs'=4] {'rhs'}, dimensions={2}, use_global_device_ids=true | all-gather | bytes 327680 | tf_op jit(solution)/shard_map/all_gather | solution.py:57
  284.3 0.0 collective-permute-done.2
  284.3 0.9 fusion.5
  285.3 0.0 all-gather.6.cloned.1.call-update
  285.3 11.2 %scatter_custom_fusion = bf16[4096,256]{1,0:T(8,128)(2,1)} fusion(s32[2048]{0:T(1024)S(1)} %bitcast.77, bf16[2048,256]{1,0:T(8,128)(2,1)} %param.11, bf16[]{:T(256)} %constant.5.clone.1), kind=kCustom, calls=%fused_computation.22 | custom fusion | bytes 2097664 | tf_op jit(solution)/shard_map/scatter | solution.py:39
  296.5 0.0 copy-done.3
  296.5 0.1 reshape.74
  296.6 0.0 copy-start.4
  296.6 5.3 %gather_fusion.1 = bf16[56,256,256]{2,1,0:T(8,128)(2,1)} fusion(bf16[8,256,256]{2,1,0:T(8,128)(2,1)S(1)} %bitcast.64, s32[1024]{0:T(1024)S(1)} %pad_clamp_fusion), kind=kCustom, calls=%fused_computation.1 | custom fusion | bytes 14680288 | tf_op jit(solution)/shard_map/gather | solution.py:28
  301.9 0.0 copy-done.4
  301.9 0.1 iota_compare_fusion.2
  302.0 8.8 %fusion = f32[8,256,256,1]{1,2,3,0:T(8,128)} fusion(bf16[8,7,256,256]{3,2,1,0:T(8,128)(2,1)} %param.13, bf16[8,7,256,256]{3,2,1,0:T(8,128)(2,1)} %bitcast.68, pred[8,7]{1,0:T(8,128)(4,1)S(1)} %iota_compare_fusion.2), kind=kOutput, calls=%fused_computation.5 | convolution fusion | flops 1882718208 | bytes 16777272 | tf_op jit(solution)/shard_map/gjab,gjbn->gan/dot_general | solution.py:31
  310.8 66.4 %all-gather.6.cloned.1.call-done = bf16[16384,256]{0,1:T(8,128)(2,1)} async-done(((bf16[256,256]{0,1:T(8,128)(2,1)}), bf16[16384,256]{0,1:T(8,128)(2,1)}) %all-gather.6.cloned.1.call-update) | async-done | bytes 8388624 | tf_op jit(solution)/shard_map/all_gather | solution.py:64
  377.1 11.9 %copy.15 = bf16[16384,256]{1,0:T(8,128)(2,1)} copy(bf16[16384,256]{0,1:T(8,128)(2,1)} %all-gather.6.cloned.1.call-done) | data formatting | bytes 16777216 | tf_op jit(solution)/shard_map/all_gather | solution.py:64
  389.0 5.6 %convolution_convert_fusion = bf16[64,64,256]{2,1,0:T(8,128)(2,1)S(1)} fusion(bf16[64,64,256]{2,1,0:T(8,128)(2,1)} %bitcast.65, bf16[64,256,256]{2,1,0:T(8,128)(2,1)} %bitcast.63), kind=kOutput, calls=%fused_computation.11 | convolution fusion | flops 537919488 | bytes 12582912 | tf_op jit(solution)/shard_map/bck,bkn->bcn/dot_general | solution.py:61
  394.6 7.5 %gather_fusion = bf16[2048,256]{1,0:T(8,128)(2,1)S(1)} fusion(bf16[4096,256]{1,0:T(8,128)(2,1)S(1)} %bitcast.62, s32[2048]{0:T(1024)S(1)} %broadcast_clamp_fusion), kind=kCustom, calls=%fused_computation | custom fusion | bytes 2105344 | tf_op jit(solution)/shard_map/gather | solution.py:70
  402.1 2.8 fusion.4
  (5 shorter events, 0.0 us)
Async XLA Ops:
  6.5 239.3 %reduce-scatter.2.cloned.1.call-start = ((), (), s32[]{:S(2)}) async-start(), calls=%async_computation.1 | async-start | bytes 17039360 | tf_op jit(solution)/shard_map/reduce_scatter | solution.py:43
  6.5 20.0 %copy-start.2 = (s32[2048,1]{0,1:T(1,128)S(1)}, s32[2048,1]{0,1:T(1,128)}, u32[]{:S(2)}) copy-start(s32[2048,1]{0,1:T(1,128)} %param.9) | copy-start | bytes 24580
  25.7 11.5 %copy-start = (bf16[2048,256]{1,0:T(8,128)(2,1)S(1)}, bf16[2048,256]{1,0:T(8,128)(2,1)}, u32[]{:S(2)}) copy-start(bf16[2048,256]{1,0:T(8,128)(2,1)} %param.8) | copy-start | bytes 3145732
  57.8 193.8 %copy-start.1 = (bf16[1,3,64,512]{3,2,1,0:T(8,128)(2,1)S(1)}, bf16[1,3,64,512]{3,2,1,0:T(8,128)(2,1)}, u32[]{:S(2)}) copy-start(bf16[1,3,64,512]{3,2,1,0:T(8,128)(2,1)} %param.12) | copy-start | bytes 589828
  57.8 319.3 %all-gather.6.cloned.1.call-start = ((), (), s32[]{:S(2)}) async-start(), calls=%async_computation.2 | async-start | bytes 8519680 | tf_op jit(solution)/shard_map/all_gather | solution.py:64
  246.8 14.7 %collective-permute-start = (bf16[256,256]{1,0:T(8,128)(2,1)S(1)}, bf16[256,256]{1,0:T(8,128)(2,1)S(1)}, u32[]{:S(2)}, u32[]{:S(2)}) collective-permute-start(bf16[256,256]{1,0:T(8,128)(2,1)S(1)} %convert_bitcast_fusion), channel_id=1, source_target_pairs={{0,4},{4,0},{8,12},{12,8},{16,20},{20,16},{24,28},{28,24},{32,36},... | collective-permute-start | bytes 393224 | tf_op jit(solution)/shard_map/ppermute | solution.py:8
  261.8 10.2 %collective-permute-start.1 = (bf16[256,256]{1,0:T(8,128)(2,1)S(1)}, bf16[256,256]{1,0:T(8,128)(2,1)S(1)}, u32[]{:S(2)}, u32[]{:S(2)}) collective-permute-start(bf16[256,256]{1,0:T(8,128)(2,1)S(1)} %fusion.6), channel_id=1, source_target_pairs={{0,8},{4,12},{8,0},{12,4},{16,24},{20,28},{24,16},{28,20},{32,40},... | collective-permute-start | bytes 393224 | tf_op jit(solution)/shard_map/ppermute | solution.py:8
  271.9 24.6 %copy-start.3 = (s32[8,7]{1,0:T(8,128)S(1)}, s32[8,7]{1,0:T(8,128)}, u32[]{:S(2)}) copy-start(s32[8,7]{1,0:T(8,128)} %param.14) | copy-start | bytes 676
  272.2 12.1 %collective-permute-start.2 = (bf16[256,256]{1,0:T(8,128)(2,1)S(1)}, bf16[256,256]{1,0:T(8,128)(2,1)S(1)}, u32[]{:S(2)}, u32[]{:S(2)}) collective-permute-start(bf16[256,256]{1,0:T(8,128)(2,1)S(1)} %fusion.7), channel_id=1, source_target_pairs={{0,16},{4,20},{8,24},{12,28},{16,0},{20,4},{24,8},{28,12},{32,48},... | collective-permute-start | bytes 393224 | tf_op jit(solution)/shard_map/ppermute | solution.py:8
  296.6 5.3 %copy-start.4 = (s32[8]{0:T(128)S(1)}, s32[8]{0:T(128)}, u32[]{:S(2)}) copy-start(s32[8]{0:T(128)} %param.15) | copy-start | bytes 100
Sparse Core Ops, SparseCore 0:
  58.0 187.8 reduce-scatter.1
  285.4 91.6 all-gather.5
where the time goes:
time: 412 us
  waiting for transfers between devices  254 us (62%)
  local copies, waits for them, and re-layouts  57.9 us (14%)
  blocking collectives  28.7 us (7%)
  matrix products  25.5 us (6%)
  other arithmetic  23.5 us (6%)
  between operations  13.5 us (3%)
  starting transfers between devices  8.35 us (2%)
    reduce_scatter x1, waiting for transfers between devices, on_device(): lax.psum_scatter(jnp.einsum('bck,bcn->bkn', v_three, x_three, preferred_e...  188 us
    all_gather x1, waiting for transfers between devices, on_device(): lax.all_gather(coefficients[None], 'leaf', axis=0, tiled=True)  66.4 us
    all_gather x3, blocking collectives, on_device(): lax.all_gather(transfer[0, level_num], 'rhs', axis=0, tiled=True)  28.7 us
    scatter x2, local copies, waits for them, and re-layouts, on_device(): jnp.zeros((n_leaf * capacity, basis_width), jnp.bfloat16).at[slot_index]  21.6 us
    another operation x3, other arithmetic  18.5 us
    all_gather x1, local copies, waits for them, and re-layouts, on_device(): lax.all_gather(coefficients[None], 'leaf', axis=0, tiled=True)  11.9 us
    scatter x1, local copies, waits for them, and re-layouts, on_device(): jnp.zeros((n_leaf * capacity, col_count), jnp.bfloat16).at[slot_index]  10.9 us
    dot_general x1, matrix products, on_device(): jnp.einsum('bck,bcn->bkn', v_three, x_three, preferred_element_type=jnp.f...  9.68 us
  transfers between devices with their start and end apart: 5, of which 2 were waited for; matrix products, arithmetic and copies ran while one was open for 6% of the time, Pallas kernels for 0%

commit v1 on v0

--- a/solution.py
+++ b/solution.py
@@ -2,6 +2,12 @@
 import jax.numpy as jnp
 from jax import lax
 from jax.sharding import PartitionSpec as P
+
+
+def tiled_gather(x, axis, dim):
+    size = lax.axis_size(axis)
+    repeats = [size if d == dim else 1 for d in range(x.ndim)]
+    return lax.all_to_all(jnp.tile(x, repeats), axis, split_axis=dim, concat_axis=dim, tiled=True)
 
 
 def swapped(value, axis, stride):
@@ -61,7 +67,7 @@
         jnp.einsum(
             "bck,bkn->bcn",
             u_three,
-            lax.all_gather(coefficients[None], "leaf", axis=0, tiled=True),
+            tiled_gather(coefficients[None], "leaf", 0),
             preferred_element_type=jnp.float32,
         )
         .astype(jnp.bfloat16)

time: 412 us -> 513 us (1.25)
  waiting for transfers between devices: 254 us -> 348 us
  starting transfers between devices: 8.35 us -> 23.3 us
  local copies, waits for them, and re-layouts: 57.9 us -> 50.3 us
    all_to_all x0 -> x1, waiting for transfers between devices: none -> 160 us  [tiled_gather(): lax.all_to_all(jnp.tile(x, repeats), axis, split_axis=dim, concat_axis=di...]
    all_gather x1 -> x0, waiting for transfers between devices: 66.4 us -> none  [on_device(): lax.all_gather(coefficients[None], 'leaf', axis=0, tiled=True)]
    all_to_all x0 -> x1, starting transfers between devices: none -> 15.2 us  [tiled_gather(): lax.all_to_all(jnp.tile(x, repeats), axis, split_axis=dim, concat_axis=di...]
    all_gather x1 -> x0, local copies, waits for them, and re-layouts: 11.9 us -> none  [on_device(): lax.all_gather(coefficients[None], 'leaf', axis=0, tiled=True)]
  transfers between devices with their start and end apart: 5 -> 5, of which waited for: 2 -> 2; matrix products, arithmetic and copies ran while one was open for 6% -> 5% of each run, Pallas kernels for 0% -> 0%
where the time goes in v1:
time: 513 us; the launch traced here: 512 us
  waiting for transfers between devices  348 us (68%)
  local copies, waits for them, and re-layouts  50.3 us (10%)
  blocking collectives  28.9 us (6%)
  matrix products  24.6 us (5%)
  other arithmetic  23.5 us (5%)
  starting transfers between devices  23.3 us (5%)
  between operations  13.5 us (3%)
    reduce_scatter x1, waiting for transfers between devices, on_device(): lax.psum_scatter(jnp.einsum('bck,bcn->bkn', v_three, x_three, preferred_e...  188 us
    all_to_all x1, waiting for transfers between devices, tiled_gather(): lax.all_to_all(jnp.tile(x, repeats), axis, split_axis=dim, concat_axis=di...  160 us
    all_gather x3, blocking collectives, on_device(): lax.all_gather(transfer[0, level_num], 'rhs', axis=0, tiled=True)  28.9 us
    scatter x2, local copies, waits for them, and re-layouts, on_device(): jnp.zeros((n_leaf * capacity, basis_width), jnp.bfloat16).at[slot_index]  21.7 us
    another operation x3, other arithmetic  18.5 us
    all_to_all x1, starting transfers between devices, tiled_gather(): lax.all_to_all(jnp.tile(x, repeats), axis, split_axis=dim, concat_axis=di...  15.2 us
    scatter x1, local copies, waits for them, and re-layouts, on_device(): jnp.zeros((n_leaf * capacity, col_count), jnp.bfloat16).at[slot_index]  10.9 us
  transfers between devices with their start and end apart: 5, of which 2 were waited for; matrix products, arithmetic and copies ran while one was open for 5% of the time, Pallas kernels for 0%

profile of v1, /device:TPU:5, one launch (start us, length us, event | category | flops | bytes accessed | tf_op | source)
XLA Modules:
  0.0 512.3 jit_solution(13008106623360762228)
XLA Ops:
  6.5 0.0 reduce-scatter.2.cloned.1.call-start
  6.5 0.0 copy-start.2
  6.5 0.8 fusion.17
  7.3 18.1 %reduce-window.6 = s32[64,16,128]{2,1,0:T(8,128)S(1)} reduce-window(s32[64,16,128]{2,1,0:T(8,128)S(1)} %fusion.17, s32[]{:T(128)} %constant.7.clone.1), window={size=1x1x128 pad=0_0x0_0x127_0}, to_apply=%region_0.0 | reduce-window | flops 16646144 | bytes 1048580 | tf_op jit(solution)/shard_map/reduce-window
  25.5 0.2 slice.24
  25.7 0.0 copy-start
  25.7 0.4 copy.12
  26.1 0.2 reduce-window.9
  26.3 0.2 broadcast_add_fusion
  26.5 0.0 copy-done.2
  26.5 0.3 fusion.16
  26.8 10.4 %scatter_custom_fusion.1 = bf16[4096,256]{1,0:T(8,128)(2,1)S(1)} fusion(s32[2048]{0:T(1024)S(1)} %bitcast.73, bf16[2048,256]{1,0:T(8,128)(2,1)} %param.10, bf16[]{:T(256)} %constant.5.clone.1), kind=kCustom, calls=%fused_computation.20 | custom fusion | bytes 2097664 | tf_op jit(solution)/shard_map/scatter | solution.py:42
  37.2 0.0 copy-done
  37.2 10.9 %scatter_custom_fusion.2 = bf16[4096,256]{1,0:T(8,128)(2,1)} fusion(s32[2048]{0:T(1024)S(1)} %bitcast.74, bf16[2048,256]{1,0:T(8,128)(2,1)S(1)} %copy-done, bf16[]{:T(256)} %constant.5.clone.1), kind=kCustom, calls=%fused_computation.18 | custom fusion | bytes 2097154 | tf_op jit(solution)/shard_map/scatter | solution.py:40
  48.1 9.7 %fusion.35 = f32[64,256,256]{2,1,0:T(8,128)} fusion(bf16[64,64,256]{2,1,0:T(8,128)(2,1)S(1)} %bitcast.64, bf16[64,64,256]{2,1,0:T(8,128)(2,1)} %bitcast.65), kind=kOutput, calls=%fused_computation.55 | convolution fusion | flops 536870912 | bytes 20971520 | tf_op jit(solution)/shard_map/bck,bcn->bkn/dot_general | solution.py:50
  57.8 0.0 copy-start.1
  57.8 0.0 reduce-scatter.2.cloned.1.call-update
  57.8 188.0 %reduce-scatter.2.cloned.1.call-done = f32[1,256,256]{2,1,0:T(8,128)} async-done(((f32[64,256,256]{2,1,0:T(8,128)}), f32[1,256,256]{2,1,0:T(8,128)}) %reduce-scatter.2.cloned.1.call-update) | async-done | bytes 262160 | tf_op jit(solution)/shard_map/reduce_scatter | solution.py:49
  245.8 1.0 convert_bitcast_fusion
  246.8 4.8 collective-permute-start
  251.6 0.0 copy-done.1
  251.6 9.9 %all-gather = bf16[1,1,256,512]{3,2,1,0:T(8,128)(2,1)S(1)} all-gather(bf16[1,1,64,512]{3,2,1,0:T(8,128)(2,1)S(1)} %get-tuple-element.6), channel_id=2, replica_groups=mesh['leaf'=64,'rhs'=4] {'rhs'}, dimensions={2}, use_global_device_ids=true | all-gather | bytes 327680 | tf_op jit(solution)/shard_map/all_gather | solution.py:63
  261.5 0.0 collective-permute-done
  261.5 0.2 fusion.5
  261.8 0.8 collective-permute-start.1
  262.6 9.4 %all-gather.1 = bf16[1,1,256,512]{3,2,1,0:T(8,128)(2,1)S(1)} all-gather(bf16[1,1,64,512]{3,2,1,0:T(8,128)(2,1)S(1)} %get-tuple-element.7), channel_id=3, replica_groups=mesh['leaf'=64,'rhs'=4] {'rhs'}, dimensions={2}, use_global_device_ids=true | all-gather | bytes 327680 | tf_op jit(solution)/shard_map/all_gather | solution.py:63
  271.9 0.0 collective-permute-done.1
  272.0 0.2 fusion.6
  272.2 2.5 collective-permute-start.2
  274.7 9.7 %all-gather.2 = bf16[1,1,256,512]{3,2,1,0:T(8,128)(2,1)S(1)} all-gather(bf16[1,1,64,512]{3,2,1,0:T(8,128)(2,1)S(1)} %get-tuple-element.5), channel_id=4, replica_groups=mesh['leaf'=64,'rhs'=4] {'rhs'}, dimensions={2}, use_global_device_ids=true | all-gather | bytes 327680 | tf_op jit(solution)/shard_map/all_gather | solution.py:63
  284.3 0.0 collective-permute-done.2
  284.3 0.2 fusion.7
  284.6 4.2 tile.2
  288.8 15.2 %all-to-all-start = ((bf16[64,256,256]{2,1,0:T(8,128)(2,1)}), bf16[64,256,256]{2,1,0:T(8,128)(2,1)}, u32[]{:S(2)}, u32[]{:S(2)}) async-start(bf16[64,256,256]{2,1,0:T(8,128)(2,1)} %tile.2), calls=%async_computation.1 | async-start | bytes 16777216 | tf_op jit(solution)/shard_map/all_to_all | solution.py:10
  304.0 0.0 copy-start.3
  304.0 11.3 %scatter_custom_fusion = bf16[4096,256]{1,0:T(8,128)(2,1)} fusion(s32[2048]{0:T(1024)S(1)} %bitcast.75, bf16[2048,256]{1,0:T(8,128)(2,1)} %param.11, bf16[]{:T(256)} %constant.5.clone.1), kind=kCustom, calls=%fused_computation.22 | custom fusion | bytes 2097664 | tf_op jit(solution)/shard_map/scatter | solution.py:45
  315.3 0.0 copy-done.3
  315.3 0.1 reshape.77
  315.4 0.0 copy-start.4
  315.4 5.2 %gather_fusion.1 = bf16[56,256,256]{2,1,0:T(8,128)(2,1)} fusion(bf16[8,256,256]{2,1,0:T(8,128)(2,1)S(1)} %bitcast.62, s32[1024]{0:T(1024)S(1)} %pad_clamp_fusion), kind=kCustom, calls=%fused_computation.1 | custom fusion | bytes 14680288 | tf_op jit(solution)/shard_map/gather | solution.py:34
  320.7 0.0 copy-done.4
  320.7 0.1 iota_compare_fusion.2
  320.8 8.6 %fusion = f32[8,256,256,1]{1,2,3,0:T(8,128)} fusion(bf16[8,7,256,256]{3,2,1,0:T(8,128)(2,1)} %param.13, bf16[8,7,256,256]{3,2,1,0:T(8,128)(2,1)} %bitcast.66, pred[8,7]{1,0:T(8,128)(4,1)S(1)} %iota_compare_fusion.2), kind=kOutput, calls=%fused_computation.5 | convolution fusion | flops 1882718208 | bytes 16777272 | tf_op jit(solution)/shard_map/gjab,gjbn->gan/dot_general | solution.py:37
  329.4 160.2 %all-to-all-done = bf16[64,256,256]{2,1,0:T(8,128)(2,1)} async-done(((bf16[64,256,256]{2,1,0:T(8,128)(2,1)}), bf16[64,256,256]{2,1,0:T(8,128)(2,1)}, u32[]{:S(2)}, u32[]{:S(2)}) %all-to-all-start) | async-done | bytes 8388640 | tf_op jit(solution)/shard_map/all_to_all | solution.py:10
  489.6 5.6 %convolution_convert_fusion = bf16[64,64,256]{2,1,0:T(8,128)(2,1)S(1)} fusion(bf16[64,64,256]{2,1,0:T(8,128)(2,1)} %bitcast.63, bf16[64,256,256]{2,1,0:T(8,128)(2,1)} %all-to-all-done), kind=kOutput, calls=%fused_computation.11 | convolution fusion | flops 537919488 | bytes 12582912 | tf_op jit(solution)/shard_map/bck,bkn->bcn/dot_general | solution.py:67
  495.2 7.5 %gather_fusion = bf16[2048,256]{1,0:T(8,128)(2,1)S(1)} fusion(bf16[4096,256]{1,0:T(8,128)(2,1)S(1)} %bitcast.61, s32[2048]{0:T(1024)S(1)} %broadcast_clamp_fusion), kind=kCustom, calls=%fused_computation | custom fusion | bytes 2105344 | tf_op jit(solution)/shard_map/gather | solution.py:76
  502.7 2.8 fusion.4
  (5 shorter events, 0.0 us)
Async XLA Ops:
  6.5 239.3 %reduce-scatter.2.cloned.1.call-start = ((), (), s32[]{:S(2)}) async-start(), calls=%async_computation.2 | async-start | bytes 17039360 | tf_op jit(solution)/shard_map/reduce_scatter | solution.py:49
  6.5 20.0 %copy-start.2 = (s32[2048,1]{0,1:T(1,128)S(1)}, s32[2048,1]{0,1:T(1,128)}, u32[]{:S(2)}) copy-start(s32[2048,1]{0,1:T(1,128)} %param.9) | copy-start | bytes 24580
  25.7 11.5 %copy-start = (bf16[2048,256]{1,0:T(8,128)(2,1)S(1)}, bf16[2048,256]{1,0:T(8,128)(2,1)}, u32[]{:S(2)}) copy-start(bf16[2048,256]{1,0:T(8,128)(2,1)} %param.8) | copy-start | bytes 3145732
  57.8 193.8 %copy-start.1 = (bf16[1,3,64,512]{3,2,1,0:T(8,128)(2,1)S(1)}, bf16[1,3,64,512]{3,2,1,0:T(8,128)(2,1)}, u32[]{:S(2)}) copy-start(bf16[1,3,64,512]{3,2,1,0:T(8,128)(2,1)} %param.12) | copy-start | bytes 589828
  246.8 14.7 %collective-permute-start = (bf16[256,256]{1,0:T(8,128)(2,1)S(1)}, bf16[256,256]{1,0:T(8,128)(2,1)S(1)}, u32[]{:S(2)}, u32[]{:S(2)}) collective-permute-start(bf16[256,256]{1,0:T(8,128)(2,1)S(1)} %convert_bitcast_fusion), channel_id=1, source_target_pairs={{0,4},{4,0},{8,12},{12,8},{16,20},{20,16},{24,28},{28,24},{32,36},... | collective-permute-start | bytes 393224 | tf_op jit(solution)/shard_map/ppermute | solution.py:14
  261.8 10.2 %collective-permute-start.1 = (bf16[256,256]{1,0:T(8,128)(2,1)S(1)}, bf16[256,256]{1,0:T(8,128)(2,1)S(1)}, u32[]{:S(2)}, u32[]{:S(2)}) collective-permute-start(bf16[256,256]{1,0:T(8,128)(2,1)S(1)} %fusion.5), channel_id=1, source_target_pairs={{0,8},{4,12},{8,0},{12,4},{16,24},{20,28},{24,16},{28,20},{32,40},... | collective-permute-start | bytes 393224 | tf_op jit(solution)/shard_map/ppermute | solution.py:14
  272.2 12.1 %collective-permute-start.2 = (bf16[256,256]{1,0:T(8,128)(2,1)S(1)}, bf16[256,256]{1,0:T(8,128)(2,1)S(1)}, u32[]{:S(2)}, u32[]{:S(2)}) collective-permute-start(bf16[256,256]{1,0:T(8,128)(2,1)S(1)} %fusion.6), channel_id=1, source_target_pairs={{0,16},{4,20},{8,24},{12,28},{16,0},{20,4},{24,8},{28,12},{32,48},... | collective-permute-start | bytes 393224 | tf_op jit(solution)/shard_map/ppermute | solution.py:14
  288.8 200.8 %all-to-all-start = ((bf16[64,256,256]{2,1,0:T(8,128)(2,1)}), bf16[64,256,256]{2,1,0:T(8,128)(2,1)}, u32[]{:S(2)}, u32[]{:S(2)}) async-start(bf16[64,256,256]{2,1,0:T(8,128)(2,1)} %tile.2), calls=%async_computation.1 | async-start | bytes 16777216 | tf_op jit(solution)/shard_map/all_to_all | solution.py:10
  304.0 11.3 %copy-start.3 = (s32[8,7]{1,0:T(8,128)S(1)}, s32[8,7]{1,0:T(8,128)}, u32[]{:S(2)}) copy-start(s32[8,7]{1,0:T(8,128)} %param.14) | copy-start | bytes 676
  315.4 5.2 %copy-start.4 = (s32[8]{0:T(128)S(1)}, s32[8]{0:T(128)}, u32[]{:S(2)}) copy-start(s32[8]{0:T(128)} %param.15) | copy-start | bytes 100
Sparse Core Ops, SparseCore 0:
  58.0 187.8 reduce-scatter.1
